TPU v7x, 256 devices: a whole 4x4x8 slice. The times are simulated.
256 devices in a mesh: tm: 32 (over x_lo, z, core), rows: 8 (over y, x_hi).
Axes of the slice: x: 4 (x_hi: 2, x_lo: 2; x = x_hi * 2 + x_lo), y: 4, z: 8, core: 2. Of those that a mesh axis runs over, the one named last changes fastest.
Arguments:
- video: bfloat16 [64, 16, 64, 384], P('tm', 'rows'), may hold values from -6 to 6
- conv_weight: bfloat16 [3, 3, 3, 384, 384], replicated, may hold values from -0.0625 to 0.0625
- norm_gain: float32 [384], replicated, may hold values from 0.1 to 1.9
- w_query: bfloat16 [384, 384], replicated, may hold values from -0.3125 to 0.3125
- w_key: bfloat16 [384, 384], replicated, may hold values from -0.875 to 0.875
- w_value: bfloat16 [384, 384], replicated, may hold values from -0.875 to 0.875
- w_out: bfloat16 [384, 384], replicated, may hold values from -0.3125 to 0.3125
- cotangent: bfloat16 [64, 16, 64, 384], P('tm', 'rows'), may hold values from -6 to 6
Outputs:
- block_out: bfloat16 [64, 16, 64, 384], P('tm', 'rows')
- video_grad: bfloat16 [64, 16, 64, 384], P('tm', 'rows')
All inputs are finite; a program needn't handle non-finite values.
Results may differ from a plain program's by a relative error of at most 0.014.
Values may be sent and summed in bfloat16 or wider, within the bound.
No kernel may reach another device: no remote copies, remote signals or barrier semaphores. Data moves between devices by JAX's collectives and lax.ppermute only.
A program may use at most 64 MiB of HBM per device.

v0:
```python
import jax
import jax.numpy as jnp
from jax import lax
from jax.sharding import PartitionSpec as P


def padded_2(cells, sides, width):
    for axis, dim in sides:
        count = lax.axis_size(axis)
        ends = count - 1
        head = lax.slice_in_dim(cells, 0, width, axis=dim)
        tail = lax.slice_in_dim(cells, cells.shape[dim] - width, cells.shape[dim], axis=dim)
        cells = jnp.concatenate(
            [
                lax.ppermute(tail, axis, [(i, (i + 1) % count) for i in range(ends)]),
                cells,
                lax.ppermute(head, axis, [((i + 1) % count, i) for i in range(ends)]),
            ],
            axis=dim,
        )
    return cells


def from_behind(value, axis, by):
    devices = lax.axis_size(axis)
    pairs = [(i, i + by) for i in range(devices) if 0 <= i + by < devices]
    return lax.ppermute(value, axis, pairs)


def convolve(padded, kernel, pads):
    result = lax.conv_general_dilated(
        padded[None],
        kernel,
        (1, 1, 1),
        pads,
        dimension_numbers=("NDHWC", "DHWIO", "NDHWC"),
        preferred_element_type=jnp.float32,
    )
    return result[0]


def project(source, weight):
    return jnp.dot(source.reshape(-1, source.shape[-1]), weight, preferred_element_type=jnp.float32)


def local(video, conv_weight, norm_gain, w_query, w_key, w_value, w_out, cotangent):
    frames, height, width, chans = video.shape
    scale = 1.0 / jnp.sqrt(jnp.float32(chans))
    rimmed = padded_2(video, (("rows", 1),), 1)
    cached = from_behind(rimmed, "tm", 1)
    extended = jnp.concatenate([cached, rimmed], axis=0)
    conv = convolve(extended, conv_weight, [(0, 0), (0, 0), (1, 1)]).astype(jnp.bfloat16)
    convf = conv.astype(jnp.float32)
    inverse = lax.rsqrt(jnp.mean(convf * convf, axis=-1, keepdims=True) + 1e-06)
    normed = convf * inverse * norm_gain
    act = jax.nn.silu(normed).astype(jnp.bfloat16)
    shape4 = (frames, height, width, chans)
    queries = project(act, w_query).astype(jnp.bfloat16).reshape(shape4)
    keys = project(act, w_key).astype(jnp.bfloat16).reshape(shape4)
    values = project(act, w_value).astype(jnp.bfloat16).reshape(shape4)
    keys_all, values_all = (
        lax.all_gather(keys, "rows", axis=1, tiled=True),
        lax.all_gather(values, "rows", axis=1, tiled=True),
    )
    query_flat = queries.reshape(frames, -1, chans)
    keys_flat = keys_all.reshape(frames, -1, chans)
    values_flat = values_all.reshape(frames, -1, chans)
    scores = (
        jnp.einsum("fqc,fkc->fqk", query_flat, keys_flat, preferred_element_type=jnp.float32)
        * scale
    )
    top = jnp.max(scores, axis=-1, keepdims=True)
    expo = jnp.exp(scores - top)
    total = jnp.sum(expo, axis=-1, keepdims=True)
    probs = expo / total
    logsum = (top + jnp.log(total))[:, :, 0]
    attended = jnp.einsum(
        "fqk,fkc->fqc", probs.astype(jnp.bfloat16), values_flat, preferred_element_type=jnp.float32
    ).astype(jnp.bfloat16)
    projected = project(attended, w_out)
    block_out = (
        (act.astype(jnp.float32).reshape(-1, chans) + projected)
        .astype(jnp.bfloat16)
        .reshape(shape4)
    )
    grad_att = project(cotangent, w_out.T).astype(jnp.bfloat16).reshape(frames, -1, chans)
    delta = jnp.sum(grad_att.astype(jnp.float32) * attended.astype(jnp.float32), axis=-1)
    probs_again = jnp.exp(scores - logsum[:, :, None])
    dprob = jnp.einsum("fqc,fkc->fqk", grad_att, values_flat, preferred_element_type=jnp.float32)
    dscore = (probs_again * (dprob - delta[:, :, None])).astype(jnp.bfloat16)
    grad_q = (
        jnp.einsum("fqk,fkc->fqc", dscore, keys_flat, preferred_element_type=jnp.float32) * scale
    ).astype(jnp.bfloat16)
    key_terms = jnp.einsum("fqk,fqc->fkc", dscore, query_flat, preferred_element_type=jnp.float32)
    value_terms = jnp.einsum(
        "fqk,fqc->fkc",
        probs_again.astype(jnp.bfloat16),
        grad_att,
        preferred_element_type=jnp.float32,
    )
    full_shape = (frames, keys_all.shape[1], width, chans)
    key_sum, value_sum = (
        lax.psum_scatter(
            key_terms.reshape(full_shape).astype(jnp.bfloat16),
            "rows",
            scatter_dimension=1,
            tiled=True,
        ).astype(jnp.float32),
        lax.psum_scatter(
            value_terms.reshape(full_shape).astype(jnp.bfloat16),
            "rows",
            scatter_dimension=1,
            tiled=True,
        ).astype(jnp.float32),
    )
    grad_k = (key_sum * scale).astype(jnp.bfloat16).reshape(frames, -1, chans)
    grad_v = value_sum.astype(jnp.bfloat16).reshape(frames, -1, chans)
    grad_act = cotangent.astype(jnp.float32).reshape(-1, chans)
    grad_act = grad_act + project(grad_q, w_query.T)
    grad_act = grad_act + project(grad_k, w_key.T)
    grad_act = grad_act + project(grad_v, w_value.T)
    grad_act = grad_act.reshape(shape4)
    sigma = jax.nn.sigmoid(normed)
    grad_normed = grad_act * sigma * (1.0 + normed * (1.0 - sigma))
    scaled = grad_normed * norm_gain
    grad_conv = inverse * (
        scaled - convf * inverse * inverse * jnp.mean(scaled * convf, axis=-1, keepdims=True)
    )
    grad_conv = grad_conv.astype(jnp.bfloat16)
    flipped = jnp.transpose(jnp.flip(conv_weight, (0, 1, 2)), (0, 1, 2, 4, 3))
    grad_padded = convolve(grad_conv, flipped, [(2, 2), (2, 2), (1, 1)])
    returned = from_behind(grad_padded[:2].astype(jnp.bfloat16), "tm", -1).astype(jnp.float32)
    grad_rimmed = grad_padded[2:]
    grad_rimmed = grad_rimmed.at[frames - 2 :].add(returned)
    from_below = from_behind(grad_rimmed[:, 0].astype(jnp.bfloat16), "rows", -1).astype(jnp.float32)
    from_above = from_behind(grad_rimmed[:, height + 1].astype(jnp.bfloat16), "rows", 1).astype(
        jnp.float32
    )
    inner = grad_rimmed[:, 1 : height + 1]
    inner = inner.at[:, height - 1].add(from_below)
    inner = inner.at[:, 0].add(from_above)
    video_grad = inner.astype(jnp.bfloat16)
    return (block_out, video_grad)


def solution(mesh):
    return jax.shard_map(
        local,
        mesh=mesh,
        in_specs=(
            P("tm", "rows", None, None),
            P(),
            P(),
            P(),
            P(),
            P(),
            P(),
            P("tm", "rows", None, None),
        ),
        out_specs=(P("tm", "rows", None, None), P("tm", "rows", None, None)),
        check_vma=False,
    )
```

profile of v0, /device:TPU:6, one launch (start us, length us, event | category | flops | bytes accessed | tf_op | source)
XLA Modules:
  0.0 364.8 jit_solution(16788286377289315291)
XLA Ops:
  7.2 1.1 fusion.51
  8.4 4.6 %collective-permute-start = (bf16[2,1,64,384]{3,2,1,0:T(8,128)(2,1)S(1)}, bf16[2,1,64,384]{3,2,1,0:T(8,128)(2,1)S(1)}, u32[]{:S(2)}, u32[]{:S(2)}) collective-permute-start(bf16[2,1,64,384]{3,2,1,0:T(8,128)(2,1)S(1)} %get-tuple-element.63), channel_id=1, source_target_pairs={{0,1},{1,2},{2,3},{3,4},{4,5},{5,6},{6,7},{8,9},{9,10},{10,11},{11... | collective-permute-start | bytes 294920 | tf_op jit(solution)/shard_map/ppermute | solution.py:15
  13.0 3.0 collective-permute-start.1
  16.6 1.0 constant_dynamic-update-slice_fusion.1
  17.6 4.3 %collective-permute-done.1 = bf16[2,1,64,384]{3,2,1,0:T(8,128)(2,1)S(1)} collective-permute-done((bf16[2,1,64,384]{3,2,1,0:T(8,128)(2,1)S(1)}, bf16[2,1,64,384]{3,2,1,0:T(8,128)(2,1)S(1)}, u32[]{:S(2)}, u32[]{:S(2)}) %collective-permute-start.1) | collective-permute-done | bytes 98336 | tf_op jit(solution)/shard_map/ppermute | solution.py:17
  21.9 1.9 collective-permute-start.2
  23.8 9.3 %collective-permute-done.2 = bf16[2,4,64,384]{3,2,1,0:T(8,128)(2,1)S(1)} collective-permute-done((bf16[2,4,64,384]{3,2,1,0:T(8,128)(2,1)S(1)}, bf16[2,4,64,384]{3,2,1,0:T(8,128)(2,1)S(1)}, u32[]{:S(2)}, u32[]{:S(2)}) %collective-permute-start.2) | collective-permute-done | bytes 393248 | tf_op jit(solution)/shard_map/ppermute | solution.py:27
  34.5 3.4 convert_multiply_fusion.2
  42.0 52.6 %all-gather.3.cloned.1.call-done = bf16[2,16,64,384]{3,2,1,0:T(8,128)(2,1)} async-done(((bf16[2,2,64,384]{3,2,1,0:T(8,128)(2,1)}), bf16[2,16,64,384]{3,2,1,0:T(8,128)(2,1)}) %all-gather.3.cloned.1.call-update) | async-done | bytes 1572880 | tf_op jit(solution)/shard_map/all_gather | solution.py:62
  94.5 2.1 fusion.52
  97.0 54.0 %all-gather.5.cloned.1.call-done = bf16[2,16,64,384]{3,2,1,0:T(8,128)(2,1)} async-done(((bf16[2,2,64,384]{3,2,1,0:T(8,128)(2,1)}), bf16[2,16,64,384]{3,2,1,0:T(8,128)(2,1)}) %all-gather.5.cloned.1.call-update) | async-done | bytes 1572880 | tf_op jit(solution)/shard_map/all_gather | solution.py:63
  151.0 2.6 multiply_reduce_fusion
  153.6 1.8 convolution_convert_fusion
  156.1 1.8 convolution_convert_fusion.1
  161.3 146.1 %all-reduce.5.cloned.1.call-done = (bf16[2,16,64,384]{3,2,1,0:T(8,128)(2,1)}, bf16[2,16,64,384]{3,2,1,0:T(8,128)(2,1)}) async-done(((bf16[2,16,64,384]{3,2,1,0:T(8,128)(2,1)}, bf16[2,16,64,384]{3,2,1,0:T(8,128)(2,1)}), (bf16[2,16,64,384]{3,2,1,0:T(8,128)(2,1)}, bf16[2,16,64,384]{3,2,1,0:T(8,128)(2,1)})) %all-reduce.5.cloned.1.call-update) | async-done | bytes 3145744
  307.4 1.0 multiply_convert_fusion.1
  310.9 17.9 %convolution_select_fusion = f32[4,4,8,9,384]{4,2,3,1,0:T(8,128)S(1)} fusion(bf16[3,3,3,384,384]{4,3,2,1,0:T(8,128)(2,1)} %param.17, pred[8,9]{0,1:T(8,128)(4,1)S(1)} %copy-done.13, bf16[2,2,1,7,2,384]{5,3,4,1,0,2:T(8,128)(2,1)S(1)} %slice.130, bf16[2,2,1,8,9,384]{5,3,4,1,0,2:T(8,128)(2,1)S(1)} %copy.100), kind=kOutput, calls=%fused_computation.4 | convolution fusion | flops 2294489088 | bytes 9996360 | tf_op jit(solution)/shard_map/conv_general_dilated | solution.py:31
  329.2 3.9 %collective-permute-start.3 = (bf16[2,4,64,384]{3,1,2,0:T(4,128)(2,1)S(1)}, bf16[2,4,64,384]{3,1,2,0:T(4,128)(2,1)S(1)}, u32[]{:S(2)}, u32[]{:S(2)}) collective-permute-start(bf16[2,4,64,384]{3,1,2,0:T(4,128)(2,1)S(1)} %slice_bitcast_fusion.1), channel_id=1, source_target_pairs={{8,0},{16,8},{24,16},{32,24},{40,32},{48,40},{56,48},{64,56},{72,6... | collective-permute-start | bytes 1179656 | tf_op jit(solution)/shard_map/ppermute | solution.py:27
  333.4 5.0 %collective-permute-done.3 = bf16[2,4,64,384]{3,1,2,0:T(4,128)(2,1)S(1)} collective-permute-done((bf16[2,4,64,384]{3,1,2,0:T(4,128)(2,1)S(1)}, bf16[2,4,64,384]{3,1,2,0:T(4,128)(2,1)S(1)}, u32[]{:S(2)}, u32[]{:S(2)}) %collective-permute-start.3) | collective-permute-done | bytes 393248 | tf_op jit(solution)/shard_map/ppermute | solution.py:27
  339.0 5.7 %collective-permute-start.4 = (bf16[2,64,384]{2,1,0:T(8,128)(2,1)S(1)}, bf16[2,64,384]{2,1,0:T(8,128)(2,1)S(1)}, u32[]{:S(2)}, u32[]{:S(2)}) collective-permute-start(bf16[2,64,384]{2,1,0:T(8,128)(2,1)S(1)} %bitcast.126), channel_id=1, source_target_pairs={{1,0},{2,1},{3,2},{4,3},{5,4},{6,5},{7,6},{9,8},{10,9},{11,10},{12... | collective-permute-start | bytes 294920 | tf_op jit(solution)/shard_map/ppermute | solution.py:27
  345.9 2.5 collective-permute-start.5
  348.8 3.2 scatter-add.6
  352.0 1.9 collective-permute-done.5
  354.1 3.2 scatter-add.9
  (93 shorter events, 16.0 us)
Async XLA Ops:
  7.2 33.0 %copy-start = (bf16[384,384]{1,0:T(8,128)(2,1)S(1)}, bf16[384,384]{1,0:T(8,128)(2,1)}, u32[]{:S(2)}) copy-start(bf16[384,384]{1,0:T(8,128)(2,1)} %param.21) | copy-start | bytes 884740
  7.2 87.4 %all-gather.3.cloned.1.call-start = ((), (), s32[]{:S(2)}) async-start(), calls=%async_computation | async-start | bytes 1769472 | tf_op jit(solution)/shard_map/all_gather | solution.py:62
  7.2 27.1 %copy-start.1 = (bf16[3,3,3,384,384]{4,3,2,1,0:T(8,128)(2,1)S(1)}, bf16[3,3,3,384,384]{4,3,2,1,0:T(8,128)(2,1)}, u32[]{:S(2)}) copy-start(bf16[3,3,3,384,384]{4,3,2,1,0:T(8,128)(2,1)} %param.17) | copy-start | bytes 23887876
  8.4 8.3 %collective-permute-start = (bf16[2,1,64,384]{3,2,1,0:T(8,128)(2,1)S(1)}, bf16[2,1,64,384]{3,2,1,0:T(8,128)(2,1)S(1)}, u32[]{:S(2)}, u32[]{:S(2)}) collective-permute-start(bf16[2,1,64,384]{3,2,1,0:T(8,128)(2,1)S(1)} %get-tuple-element.63), channel_id=1, source_target_pairs={{0,1},{1,2},{2,3},{3,4},{4,5},{5,6},{6,7},{8,9},{9,10},{10,11},{11... | collective-permute-start | bytes 294920 | tf_op jit(solution)/shard_map/ppermute | solution.py:15
  13.0 8.9 %collective-permute-start.1 = (bf16[2,1,64,384]{3,2,1,0:T(8,128)(2,1)S(1)}, bf16[2,1,64,384]{3,2,1,0:T(8,128)(2,1)S(1)}, u32[]{:S(2)}, u32[]{:S(2)}) collective-permute-start(bf16[2,1,64,384]{3,2,1,0:T(8,128)(2,1)S(1)} %get-tuple-element.62), channel_id=1, source_target_pairs={{1,0},{2,1},{3,2},{4,3},{5,4},{6,5},{7,6},{9,8},{10,9},{11,10},{12... | collective-permute-start | bytes 294920 | tf_op jit(solution)/shard_map/ppermute | solution.py:17
  21.9 11.2 %collective-permute-start.2 = (bf16[2,4,64,384]{3,2,1,0:T(8,128)(2,1)S(1)}, bf16[2,4,64,384]{3,2,1,0:T(8,128)(2,1)S(1)}, u32[]{:S(2)}, u32[]{:S(2)}) collective-permute-start(bf16[2,4,64,384]{3,2,1,0:T(8,128)(2,1)S(1)} %constant_dynamic-update-slice_fusion), channel_id=1, source_target_pairs={{0,8},{8,16},{16,24},{24,32},{32,40},{40,48},{48,56},{56,64},{64,7... | collective-permute-start | bytes 1179656 | tf_op jit(solution)/shard_map/ppermute | solution.py:27
  33.8 0.7 copy-start.13
  37.9 1.1 copy-start.12
  37.9 1.2 copy-start.4
  38.5 2.9 copy-start.5
  38.5 2.9 copy-start.9
  38.7 3.0 copy-start.7
  40.1 110.9 %all-gather.5.cloned.1.call-start = ((), (), s32[]{:S(2)}) async-start(), calls=%async_computation.1 | async-start | bytes 1769472 | tf_op jit(solution)/shard_map/all_gather | solution.py:63
  41.1 266.2 %all-reduce.5.cloned.1.call-start = ((), (), s32[]{:S(2)}) async-start(), calls=%async_computation.2 | async-start | bytes 6291456
  153.6 1.8 copy-start.3
  157.9 0.7 copy-start.14
  157.9 2.2 copy-start.2
  159.9 1.0 copy-start.8
  160.0 1.0 copy-start.10
  329.2 9.2 %collective-permute-start.3 = (bf16[2,4,64,384]{3,1,2,0:T(4,128)(2,1)S(1)}, bf16[2,4,64,384]{3,1,2,0:T(4,128)(2,1)S(1)}, u32[]{:S(2)}, u32[]{:S(2)}) collective-permute-start(bf16[2,4,64,384]{3,1,2,0:T(4,128)(2,1)S(1)} %slice_bitcast_fusion.1), channel_id=1, source_target_pairs={{8,0},{16,8},{24,16},{32,24},{40,32},{48,40},{56,48},{64,56},{72,6... | collective-permute-start | bytes 1179656 | tf_op jit(solution)/shard_map/ppermute | solution.py:27
  338.4 6.3 %copy-start.6 = (bf16[384,384]{1,0:T(8,128)(2,1)S(1)}, bf16[384,384]{1,0:T(8,128)(2,1)}, u32[]{:S(2)}) copy-start(bf16[384,384]{1,0:T(8,128)(2,1)} %param.22) | copy-start | bytes 884740
  338.4 6.3 %copy-start.11 = (bf16[2,128,384]{2,1,0:T(8,128)(2,1)S(1)}, bf16[2,128,384]{2,1,0:T(8,128)(2,1)}, u32[]{:S(2)}) copy-start(bf16[2,128,384]{2,1,0:T(8,128)(2,1)} %get-tuple-element.69) | copy-start | bytes 589828
  339.0 9.5 %collective-permute-start.4 = (bf16[2,64,384]{2,1,0:T(8,128)(2,1)S(1)}, bf16[2,64,384]{2,1,0:T(8,128)(2,1)S(1)}, u32[]{:S(2)}, u32[]{:S(2)}) collective-permute-start(bf16[2,64,384]{2,1,0:T(8,128)(2,1)S(1)} %bitcast.126), channel_id=1, source_target_pairs={{1,0},{2,1},{3,2},{4,3},{5,4},{6,5},{7,6},{9,8},{10,9},{11,10},{12... | collective-permute-start | bytes 294920 | tf_op jit(solution)/shard_map/ppermute | solution.py:27
  345.9 8.0 %collective-permute-start.5 = (bf16[2,64,384]{2,1,0:T(8,128)(2,1)S(1)}, bf16[2,64,384]{2,1,0:T(8,128)(2,1)S(1)}, u32[]{:S(2)}, u32[]{:S(2)}) collective-permute-start(bf16[2,64,384]{2,1,0:T(8,128)(2,1)S(1)} %bitcast.127), channel_id=1, source_target_pairs={{0,1},{1,2},{2,3},{3,4},{4,5},{5,6},{6,7},{8,9},{9,10},{10,11},{11... | collective-permute-start | bytes 294920 | tf_op jit(solution)/shard_map/ppermute | solution.py:27
Sparse Core Ops, SparseCore 0:
  40.2 54.2 all-gather.2
  97.7 53.2 all-gather.4
  158.0 149.3 all-reduce.4
where the time goes:
time: 365 us
  waiting for transfers between devices  274 us (75%)
  matrix products  35.1 us (10%)
  starting transfers between devices  22 us (6%)
  local copies, waits for them, and re-layouts  15.9 us (4%)
  between operations  15 us (4%)
    unnamed x4, waiting for transfers between devices  146 us
    all_gather x1, waiting for transfers between devices, local(): lax.all_gather(values, 'rows', axis=1, tiled=True)  54 us
    all_gather x1, waiting for transfers between devices, local(): lax.all_gather(keys, 'rows', axis=1, tiled=True)  52.6 us
    conv_general_dilated x2, matrix products, convolve(): lax.conv_general_dilated(padded[None], kernel, (1, 1, 1), pads, dimension...  21.3 us
    ppermute x4, waiting for transfers between devices, from_behind(): return lax.ppermute(value, axis, pairs)  16.1 us
    ppermute x4, starting transfers between devices, from_behind(): return lax.ppermute(value, axis, pairs)  14.1 us
  transfers between devices with their start and end apart: 9, of which 8 were waited for; matrix products, arithmetic and copies ran while one was open for 3% of the time, Pallas kernels for 0%

commit v1 on v0

--- a/solution.py
+++ b/solution.py
@@ -60,7 +60,9 @@
     values = project(act, w_value).astype(jnp.bfloat16).reshape(shape4)
     keys_all, values_all = (
         lax.all_gather(keys, "rows", axis=1, tiled=True),
-        lax.all_gather(values, "rows", axis=1, tiled=True),
+        jnp.concatenate(
+            lax.all_to_all(jnp.stack([values] * lax.axis_size("rows")), "rows", 0, 0), axis=1
+        ),
     )
     query_flat = queries.reshape(frames, -1, chans)
     keys_flat = keys_all.reshape(frames, -1, chans)

time: 365 us -> 316 us (0.87)
  waiting for transfers between devices: 274 us -> 216 us
  starting transfers between devices: 22 us -> 29 us
    all_gather x1 -> x0, waiting for transfers between devices: 54 us -> none  [local(): lax.all_gather(values, 'rows', axis=1, tiled=True)]
    all_gather x1, waiting for transfers between devices: 52.6 us -> 30.3 us  [local(): lax.all_gather(keys, 'rows', axis=1, tiled=True)]
    all_to_all x0 -> x1, waiting for transfers between devices: none -> 18.7 us  [local(): lax.all_to_all(jnp.stack([values] * lax.axis_size('rows')), 'rows', 0, 0)]
    all_to_all x0 -> x1, starting transfers between devices: none -> 7.28 us  [local(): lax.all_to_all(jnp.stack([values] * lax.axis_size('rows')), 'rows', 0, 0)]
    unnamed x4 -> x3, waiting for transfers between devices: 146 us -> 146 us
  transfers between devices with their start and end apart: 9 -> 9, of which waited for: 8 -> 8; matrix products, arithmetic and copies ran while one was open for 3% -> 4% of each run, Pallas kernels for 0% -> 0%
where the time goes in v1:
time: 316 us
  waiting for transfers between devices  216 us (68%)
  matrix products  34 us (11%)
  starting transfers between devices  29 us (9%)
  local copies, waits for them, and re-layouts  18.1 us (6%)
  between operations  15.3 us (5%)
    unnamed x3, waiting for transfers between devices  146 us
    all_gather x1, waiting for transfers between devices, local(): lax.all_gather(keys, 'rows', axis=1, tiled=True)  30.3 us
    conv_general_dilated x2, matrix products, convolve(): lax.conv_general_dilated(padded[None], kernel, (1, 1, 1), pads, dimension...  21.3 us
    all_to_all x1, waiting for transfers between devices, local(): lax.all_to_all(jnp.stack([values] * lax.axis_size('rows')), 'rows', 0, 0)  18.7 us
    ppermute x4, waiting for transfers between devices, from_behind(): return lax.ppermute(value, axis, pairs)  16.1 us
    ppermute x4, starting transfers between devices, from_behind(): return lax.ppermute(value, axis, pairs)  14.1 us
    all_to_all x1, starting transfers between devices, local(): lax.all_to_all(jnp.stack([values] * lax.axis_size('rows')), 'rows', 0, 0)  7.28 us
  transfers between devices with their start and end apart: 9, of which 8 were waited for; matrix products, arithmetic and copies ran while one was open for 4% of the time, Pallas kernels for 0%

profile of v1, /device:TPU:6, one launch (start us, length us, event | category | flops | bytes accessed | tf_op | source)
XLA Modules:
  0.0 315.6 jit_solution(6890522990548540437)
XLA Ops:
  7.2 1.1 fusion.51
  8.4 4.6 %collective-permute-start = (bf16[2,1,64,384]{3,2,1,0:T(8,128)(2,1)S(1)}, bf16[2,1,64,384]{3,2,1,0:T(8,128)(2,1)S(1)}, u32[]{:S(2)}, u32[]{:S(2)}) collective-permute-start(bf16[2,1,64,384]{3,2,1,0:T(8,128)(2,1)S(1)} %get-tuple-element.63), channel_id=1, source_target_pairs={{0,1},{1,2},{2,3},{3,4},{4,5},{5,6},{6,7},{8,9},{9,10},{10,11},{11... | collective-permute-start | bytes 294920 | tf_op jit(solution)/shard_map/ppermute | solution.py:15
  13.0 3.0 collective-permute-start.1
  17.6 4.3 %collective-permute-done.1 = bf16[2,1,64,384]{3,2,1,0:T(8,128)(2,1)S(1)} collective-permute-done((bf16[2,1,64,384]{3,2,1,0:T(8,128)(2,1)S(1)}, bf16[2,1,64,384]{3,2,1,0:T(8,128)(2,1)S(1)}, u32[]{:S(2)}, u32[]{:S(2)}) %collective-permute-start.1) | collective-permute-done | bytes 98336 | tf_op jit(solution)/shard_map/ppermute | solution.py:17
  21.9 1.9 collective-permute-start.2
  23.8 9.3 %collective-permute-done.2 = bf16[2,4,64,384]{3,2,1,0:T(8,128)(2,1)S(1)} collective-permute-done((bf16[2,4,64,384]{3,2,1,0:T(8,128)(2,1)S(1)}, bf16[2,4,64,384]{3,2,1,0:T(8,128)(2,1)S(1)}, u32[]{:S(2)}, u32[]{:S(2)}) %collective-permute-start.2) | collective-permute-done | bytes 393248 | tf_op jit(solution)/shard_map/ppermute | solution.py:27
  34.5 3.4 %convert_multiply_fusion.2 = (f32[2,2,8,9,384]{4,2,3,1,0:T(8,128)S(1)}, bf16[2,2,8,9,384]{4,2,3,1,0:T(8,128)(2,1)S(1)}) fusion(bf16[3,3,3,384,384]{4,3,2,1,0:T(8,128)(2,1)S(1)} %copy-done.1, bf16[4,4,1,7,2,384]{5,3,4,1,0,2:T(8,128)(2,1)S(1)} %slice.126, bf16[4,4,1,8,9,384]{5,3,4,1,0,2:T(8,128)(2,1)S(1)} %copy.90, pred[8,9]{0,1:T(8,128)(4,1)S(1)} %copy-done.20), kind=kOutput, calls=%fused_computation.73 | convolution fusion | flops 2296922112 | bytes 9683016 | tf_op jit(solution)/shard_map/conv_general_dilated | solution.py:31
  40.7 1.4 stack.3
  42.1 7.3 %all-to-all-start = ((bf16[8,2,2,64,384]{4,3,2,1,0:T(8,128)(2,1)}), bf16[8,2,2,64,384]{4,3,2,1,0:T(8,128)(2,1)S(1)}, u32[]{:S(2)}, u32[]{:S(2)}) async-start(bf16[8,2,2,64,384]{4,3,2,1,0:T(8,128)(2,1)} %stack.3), calls=%async_computation | async-start | bytes 3145728 | tf_op jit(solution)/shard_map/all_to_all | solution.py:64
  49.4 1.0 convolution_convert_fusion.3
  51.3 18.7 %all-to-all-done = bf16[8,2,2,64,384]{4,3,2,1,0:T(8,128)(2,1)S(1)} async-done(((bf16[8,2,2,64,384]{4,3,2,1,0:T(8,128)(2,1)}), bf16[8,2,2,64,384]{4,3,2,1,0:T(8,128)(2,1)S(1)}, u32[]{:S(2)}, u32[]{:S(2)}) %all-to-all-start) | async-done | bytes 1572896 | tf_op jit(solution)/shard_map/all_to_all | solution.py:64
  70.2 30.3 %all-gather.2.cloned.1.call-done = bf16[2,16,64,384]{3,2,1,0:T(8,128)(2,1)} async-done(((bf16[2,2,64,384]{3,2,1,0:T(8,128)(2,1)}), bf16[2,16,64,384]{3,2,1,0:T(8,128)(2,1)}) %all-gather.2.cloned.1.call-update) | async-done | bytes 1572880 | tf_op jit(solution)/shard_map/all_gather | solution.py:62
  100.6 2.3 fusion.52
  103.8 1.9 convolution_convert_fusion
  106.6 1.8 convolution_convert_fusion.1
  111.8 146.1 %all-reduce.5.cloned.1.call-done = (bf16[2,16,64,384]{3,2,1,0:T(8,128)(2,1)}, bf16[2,16,64,384]{3,2,1,0:T(8,128)(2,1)}) async-done(((bf16[2,16,64,384]{3,2,1,0:T(8,128)(2,1)}, bf16[2,16,64,384]{3,2,1,0:T(8,128)(2,1)}), (bf16[2,16,64,384]{3,2,1,0:T(8,128)(2,1)}, bf16[2,16,64,384]{3,2,1,0:T(8,128)(2,1)})) %all-reduce.5.cloned.1.call-update) | async-done | bytes 3145744
  261.5 17.9 %convolution_select_fusion = f32[4,4,8,9,384]{4,2,3,1,0:T(8,128)S(1)} fusion(bf16[3,3,3,384,384]{4,3,2,1,0:T(8,128)(2,1)} %param.17, pred[8,9]{0,1:T(8,128)(4,1)S(1)} %copy-done.20, bf16[2,2,1,7,2,384]{5,3,4,1,0,2:T(8,128)(2,1)S(1)} %slice.130, bf16[2,2,1,8,9,384]{5,3,4,1,0,2:T(8,128)(2,1)S(1)} %copy.102), kind=kOutput, calls=%fused_computation.4 | convolution fusion | flops 2294489088 | bytes 9996360 | tf_op jit(solution)/shard_map/conv_general_dilated | solution.py:31
  279.8 3.9 %collective-permute-start.3 = (bf16[2,4,64,384]{3,1,2,0:T(4,128)(2,1)S(1)}, bf16[2,4,64,384]{3,1,2,0:T(4,128)(2,1)S(1)}, u32[]{:S(2)}, u32[]{:S(2)}) collective-permute-start(bf16[2,4,64,384]{3,1,2,0:T(4,128)(2,1)S(1)} %slice_bitcast_fusion.1), channel_id=1, source_target_pairs={{8,0},{16,8},{24,16},{32,24},{40,32},{48,40},{56,48},{64,56},{72,6... | collective-permute-start | bytes 1179656 | tf_op jit(solution)/shard_map/ppermute | solution.py:27
  284.0 5.0 %collective-permute-done.3 = bf16[2,4,64,384]{3,1,2,0:T(4,128)(2,1)S(1)} collective-permute-done((bf16[2,4,64,384]{3,1,2,0:T(4,128)(2,1)S(1)}, bf16[2,4,64,384]{3,1,2,0:T(4,128)(2,1)S(1)}, u32[]{:S(2)}, u32[]{:S(2)}) %collective-permute-start.3) | collective-permute-done | bytes 393248 | tf_op jit(solution)/shard_map/ppermute | solution.py:27
  289.5 5.7 %collective-permute-start.4 = (bf16[2,64,384]{2,1,0:T(8,128)(2,1)S(1)}, bf16[2,64,384]{2,1,0:T(8,128)(2,1)S(1)}, u32[]{:S(2)}, u32[]{:S(2)}) collective-permute-start(bf16[2,64,384]{2,1,0:T(8,128)(2,1)S(1)} %bitcast.128), channel_id=1, source_target_pairs={{1,0},{2,1},{3,2},{4,3},{5,4},{6,5},{7,6},{9,8},{10,9},{11,10},{12... | collective-permute-start | bytes 294920 | tf_op jit(solution)/shard_map/ppermute | solution.py:27
  296.5 2.5 collective-permute-start.5
  299.4 3.2 %scatter-add.6 = f32[2,2,64,384]{3,1,2,0:T(2,128)S(1)} dynamic-update-slice(f32[2,2,64,384]{3,1,2,0:T(2,128)S(1)} %slice.135, f32[2,1,64,384]{3,1,2,0:T(1,128)S(1)} %slice_add_fusion.1, s32[]{:T(128)} %constant.106.clone.1, s32[]{:T(128)} %constant.107.clone.1, s32[]{:T(128)} %constant.106.clone.1, s32[]{:T(128)} %constant.106.clone.1) | dynamic-update-slice | bytes 393220 | tf_op jit(solution)/shard_map/scatter-add | solution.py:142
  302.6 1.9 collective-permute-done.5
  304.7 3.2 %scatter-add.9 = f32[2,2,64,384]{3,1,2,0:T(2,128)S(1)} dynamic-update-slice(f32[2,2,64,384]{3,1,2,0:T(2,128)S(1)} %scatter-add.6, f32[2,1,64,384]{3,1,2,0:T(1,128)S(1)} %slice_add_fusion, s32[]{:T(128)} %constant.106.clone.1, s32[]{:T(128)} %constant.106.clone.1, s32[]{:T(128)} %constant.106.clone.1, s32[]{:T(128)} %constant.106.clone.1) | dynamic-update-slice | bytes 393220 | tf_op jit(solution)/shard_map/scatter-add | solution.py:143
  (108 shorter events, 18.7 us)
Async XLA Ops:
  7.2 33.2 %copy-start = (bf16[384,384]{1,0:T(8,128)(2,1)S(1)}, bf16[384,384]{1,0:T(8,128)(2,1)}, u32[]{:S(2)}) copy-start(bf16[384,384]{1,0:T(8,128)(2,1)} %param.21) | copy-start | bytes 884740
  7.2 93.4 %all-gather.2.cloned.1.call-start = ((), (), s32[]{:S(2)}) async-start(), calls=%async_computation.1 | async-start | bytes 1769472 | tf_op jit(solution)/shard_map/all_gather | solution.py:62
  7.2 27.1 %copy-start.1 = (bf16[3,3,3,384,384]{4,3,2,1,0:T(8,128)(2,1)S(1)}, bf16[3,3,3,384,384]{4,3,2,1,0:T(8,128)(2,1)}, u32[]{:S(2)}) copy-start(bf16[3,3,3,384,384]{4,3,2,1,0:T(8,128)(2,1)} %param.17) | copy-start | bytes 23887876
  8.4 8.3 %collective-permute-start = (bf16[2,1,64,384]{3,2,1,0:T(8,128)(2,1)S(1)}, bf16[2,1,64,384]{3,2,1,0:T(8,128)(2,1)S(1)}, u32[]{:S(2)}, u32[]{:S(2)}) collective-permute-start(bf16[2,1,64,384]{3,2,1,0:T(8,128)(2,1)S(1)} %get-tuple-element.63), channel_id=1, source_target_pairs={{0,1},{1,2},{2,3},{3,4},{4,5},{5,6},{6,7},{8,9},{9,10},{10,11},{11... | collective-permute-start | bytes 294920 | tf_op jit(solution)/shard_map/ppermute | solution.py:15
  13.0 8.9 %collective-permute-start.1 = (bf16[2,1,64,384]{3,2,1,0:T(8,128)(2,1)S(1)}, bf16[2,1,64,384]{3,2,1,0:T(8,128)(2,1)S(1)}, u32[]{:S(2)}, u32[]{:S(2)}) collective-permute-start(bf16[2,1,64,384]{3,2,1,0:T(8,128)(2,1)S(1)} %get-tuple-element.62), channel_id=1, source_target_pairs={{1,0},{2,1},{3,2},{4,3},{5,4},{6,5},{7,6},{9,8},{10,9},{11,10},{12... | collective-permute-start | bytes 294920 | tf_op jit(solution)/shard_map/ppermute | solution.py:17
  21.9 11.2 %collective-permute-start.2 = (bf16[2,4,64,384]{3,2,1,0:T(8,128)(2,1)S(1)}, bf16[2,4,64,384]{3,2,1,0:T(8,128)(2,1)S(1)}, u32[]{:S(2)}, u32[]{:S(2)}) collective-permute-start(bf16[2,4,64,384]{3,2,1,0:T(8,128)(2,1)S(1)} %constant_dynamic-update-slice_fusion), channel_id=1, source_target_pairs={{0,8},{8,16},{16,24},{24,32},{32,40},{40,48},{48,56},{56,64},{64,7... | collective-permute-start | bytes 1179656 | tf_op jit(solution)/shard_map/ppermute | solution.py:27
  37.9 1.5 copy-start.7
  38.6 2.1 copy-start.15
  39.4 10.9 %copy-start.3 = (bf16[256,384]{1,0:T(8,128)(2,1)}, bf16[256,384]{1,0:T(8,128)(2,1)S(1)}, u32[]{:S(2)}) copy-start(bf16[256,384]{1,0:T(8,128)(2,1)S(1)} %fusion.28) | copy-start | bytes 589828
  42.1 7.3 %copy-start.9 = (bf16[384,384]{1,0:T(8,128)(2,1)S(1)}, bf16[384,384]{1,0:T(8,128)(2,1)}, u32[]{:S(2)}) copy-start(bf16[384,384]{1,0:T(8,128)(2,1)} %param.22) | copy-start | bytes 884740
  42.1 7.3 %copy-start.17 = (bf16[2,2,64,384]{3,2,1,0:T(8,128)(2,1)S(1)}, bf16[2,2,64,384]{3,2,1,0:T(8,128)(2,1)}, u32[]{:S(2)}) copy-start(bf16[2,2,64,384]{3,2,1,0:T(8,128)(2,1)} %param.23) | copy-start | bytes 589828
  42.1 8.3 %copy-start.11 = (bf16[384,384]{1,0:T(8,128)(2,1)S(1)}, bf16[384,384]{1,0:T(8,128)(2,1)}, u32[]{:S(2)}) copy-start(bf16[384,384]{1,0:T(8,128)(2,1)} %param.19) | copy-start | bytes 884740
  42.1 27.9 %all-to-all-start = ((bf16[8,2,2,64,384]{4,3,2,1,0:T(8,128)(2,1)}), bf16[8,2,2,64,384]{4,3,2,1,0:T(8,128)(2,1)S(1)}, u32[]{:S(2)}, u32[]{:S(2)}) async-start(bf16[8,2,2,64,384]{4,3,2,1,0:T(8,128)(2,1)} %stack.3), calls=%async_computation | async-start | bytes 3145728 | tf_op jit(solution)/shard_map/all_to_all | solution.py:64
  49.4 208.5 %all-reduce.5.cloned.1.call-start = ((), (), s32[]{:S(2)}) async-start(), calls=%async_computation.2 | async-start | bytes 6291456
  100.6 2.6 copy-start.6
  108.4 1.9 copy-start.14
  108.4 2.2 copy-start.2
  110.6 149.2 %copy-start.8 = (bf16[384,384]{1,0:T(8,128)(2,1)S(1)}, bf16[384,384]{1,0:T(8,128)(2,1)}, u32[]{:S(2)}) copy-start(bf16[384,384]{1,0:T(8,128)(2,1)} %param.20) | copy-start | bytes 884740
  111.5 148.6 %copy-start.16 = (bf16[2,2,1,64,384]{4,3,2,1,0:T(8,128)(2,1)S(1)}, bf16[2,2,1,64,384]{4,3,2,1,0:T(8,128)(2,1)}, u32[]{:S(2)}) copy-start(bf16[2,2,1,64,384]{4,3,2,1,0:T(8,128)(2,1)} %copy-done.15) | copy-start | bytes 589828
  279.8 9.2 %collective-permute-start.3 = (bf16[2,4,64,384]{3,1,2,0:T(4,128)(2,1)S(1)}, bf16[2,4,64,384]{3,1,2,0:T(4,128)(2,1)S(1)}, u32[]{:S(2)}, u32[]{:S(2)}) collective-permute-start(bf16[2,4,64,384]{3,1,2,0:T(4,128)(2,1)S(1)} %slice_bitcast_fusion.1), channel_id=1, source_target_pairs={{8,0},{16,8},{24,16},{32,24},{40,32},{48,40},{56,48},{64,56},{72,6... | collective-permute-start | bytes 1179656 | tf_op jit(solution)/shard_map/ppermute | solution.py:27
  289.0 6.3 %copy-start.4 = (bf16[256,384]{1,0:T(8,128)(2,1)S(1)}, bf16[256,384]{1,0:T(8,128)(2,1)}, u32[]{:S(2)}) copy-start(bf16[256,384]{1,0:T(8,128)(2,1)} %copy-done.3) | copy-start | bytes 589828
  289.0 6.3 %copy-start.10 = (bf16[384,384]{1,0:T(8,128)(2,1)S(1)}, bf16[384,384]{1,0:T(8,128)(2,1)}, u32[]{:S(2)}) copy-start(bf16[384,384]{1,0:T(8,128)(2,1)} %param.22) | copy-start | bytes 884740
  289.5 9.5 %collective-permute-start.4 = (bf16[2,64,384]{2,1,0:T(8,128)(2,1)S(1)}, bf16[2,64,384]{2,1,0:T(8,128)(2,1)S(1)}, u32[]{:S(2)}, u32[]{:S(2)}) collective-permute-start(bf16[2,64,384]{2,1,0:T(8,128)(2,1)S(1)} %bitcast.128), channel_id=1, source_target_pairs={{1,0},{2,1},{3,2},{4,3},{5,4},{6,5},{7,6},{9,8},{10,9},{11,10},{12... | collective-permute-start | bytes 294920 | tf_op jit(solution)/shard_map/ppermute | solution.py:27
  296.5 8.0 %collective-permute-start.5 = (bf16[2,64,384]{2,1,0:T(8,128)(2,1)S(1)}, bf16[2,64,384]{2,1,0:T(8,128)(2,1)S(1)}, u32[]{:S(2)}, u32[]{:S(2)}) collective-permute-start(bf16[2,64,384]{2,1,0:T(8,128)(2,1)S(1)} %bitcast.129), channel_id=1, source_target_pairs={{0,1},{1,2},{2,3},{3,4},{4,5},{5,6},{6,7},{8,9},{9,10},{10,11},{11... | collective-permute-start | bytes 294920 | tf_op jit(solution)/shard_map/ppermute | solution.py:27
  (7 other events, 6.3 us)
Sparse Core Ops, SparseCore 0:
  40.5 60.0 all-gather.1
  108.5 149.3 all-reduce.4
